TPU v7x, 32 devices: a whole 2x2x4 slice. The times are simulated.
32 devices in a mesh: tm: 16 (over z, y, x), region: 2 (over core).
Axes of the slice: x: 2, y: 2, z: 4, core: 2. Of those that a mesh axis runs over, the one named last changes fastest.
Arguments:
- cost: bfloat16 [384, 24, 1024], P('tm', 'region'), may hold values from -25 to 25
- demand: bfloat16 [384, 24, 256], P('tm', 'region'), may hold values from -25 to 25
- conversion: float32 [1024, 256], replicated, may hold values from -0.1875 to 0.1875
- upper: float32 [24, 1024], P('region'), may hold values from 0.2 to 2
- decay: float32 [384, 24, 128], P('tm', 'region'), may hold values from 0.4 to 1
- energy_cap: float32 [24, 128], P('region'), may hold values from 0.02 to 0.4
- annual_cap: float32 [24, 1024], P('region'), may hold values from 0.05 to 1
- line_ends: int32 [64, 2], P('region'), may hold values from 0 to 23, as said below
- line_cap: float32 [64], P('region'), may hold values from 0.2 to 2
Outputs:
- primal: bfloat16 [384, 24, 1024], P('tm', 'region')
- flows: float32 [384, 64], P('tm', 'region')
- prices: float32 [384, 24, 256], P('tm', 'region')
- storage_dual: float32 [384, 24, 128], P('tm', 'region')
- year_dual: float32 [24, 1024], P('region')
Inputs may be any that keep to these rules, and one draw needn't show every extreme that they name: `line_ends`: each line joins two different regions, every region is the first end of some line.
All inputs are finite; a program needn't handle non-finite values.
Results may differ from a plain program's by a relative error of at most 0.0012.
Values sent between devices are 32-bit elements; how exact they have to be, the bound alone decides.
A program may use at most 64 MiB of HBM per device.

v0:
```python
import math

import jax
import jax.numpy as jnp
from jax import lax
from jax.sharding import PartitionSpec as P

ITERS = 2


step_ratio = 0.5


def carried_in(part, axis, combine, identity, reverse):
    count = lax.axis_size(axis)
    place = lax.axis_index(axis)
    ahead = count - 1 - place if reverse else place
    gathered = jax.tree.map(lambda a: lax.all_gather(a, axis), part)
    state = jax.tree.map(lambda a, e: jnp.zeros_like(a) + jnp.asarray(e, a.dtype), part, identity)

    def one(hop, state):
        source = count - 1 - hop if reverse else hop
        return combine(
            state, jax.tree.map(lambda a: lax.dynamic_index_in_dim(a, source, 0, False), gathered)
        )

    return lax.fori_loop(0, ahead, one, state)


def affine(earlier, later):
    return (earlier[0] * later[0], later[0] * earlier[1] + later[1])


def per_device(cost, demand, conversion, upper, decay, energy_cap, annual_cap, line_ends, line_cap):
    highest = lax.Precision.HIGHEST
    hours_dev, regions_dev, width = cost.shape
    rows_bus = demand.shape[2]
    units = decay.shape[2]
    lines_dev = line_ends.shape[0]
    time_count = lax.axis_size("tm")
    group_count = lax.axis_size("region")
    hours_all = hours_dev * time_count
    regions_all = regions_dev * group_count
    level_scale = 1.0 / math.sqrt(hours_all)
    year_scale = 1.0 / math.sqrt(hours_all)
    year_bound = math.sqrt(hours_all)
    costs = cost.astype(jnp.float32)
    loads = demand.astype(jnp.float32)
    squares = lax.psum((jnp.sum(costs * costs), jnp.sum(loads * loads)), ("tm", "region"))
    omega = jnp.sqrt(squares[0] / squares[1])
    tau_step = step_ratio / omega
    sigma_step = step_ratio * omega
    columns = jnp.arange(width, dtype=jnp.int32)
    lower = jnp.where(columns[None, :] < units, -upper, jnp.float32(0.0))
    region_ids = jnp.arange(regions_all, dtype=jnp.int32)
    incidence = (line_ends[:, 1:2] == region_ids[None, :]).astype(jnp.float32) - (
        line_ends[:, 0:1] == region_ids[None, :]
    ).astype(jnp.float32)
    identity = (
        jnp.ones((regions_dev, units), jnp.float32),
        jnp.zeros((regions_dev, units), jnp.float32),
    )
    primal = jnp.zeros((hours_dev, regions_dev, width), jnp.float32)
    flows = jnp.zeros((hours_dev, lines_dev), jnp.float32)
    prices = jnp.zeros((hours_dev, regions_dev, rows_bus), jnp.float32)
    storage_dual = jnp.zeros((hours_dev, regions_dev, units), jnp.float32)
    year_dual = jnp.zeros((regions_dev, width), jnp.float32)
    for step in range(ITERS):
        if step == 0:
            grad = costs
            flow_grad = jnp.zeros_like(flows)
        else:
            back = jnp.dot(prices.reshape(-1, rows_bus), conversion.T, precision=highest).reshape(
                hours_dev, regions_dev, width
            )
            weighted = level_scale * storage_dual
            scale_run, offset_run = lax.associative_scan(
                affine, (decay, decay * weighted), axis=0, reverse=True
            )
            closing_output = carried_in((scale_run[0], offset_run[0]), "tm", affine, identity, True)
            full_run = offset_run + scale_run * closing_output[1][None]
            stored = jnp.pad(
                weighted + jnp.concatenate([full_run[1:], closing_output[1][None]], axis=0),
                ((0, 0), (0, 0), (0, width - units)),
            )
            grad = costs + back + stored + year_scale * year_dual[None]
            bus = lax.all_gather(prices[:, :, 0], "region", axis=1, tiled=True)
            flow_grad = jnp.dot(bus, incidence.T, precision=highest)
        new_primal = jnp.clip(primal - tau_step * grad, lower[None], upper[None])
        new_flows = jnp.clip(flows - tau_step * flow_grad, -line_cap[None], line_cap[None])
        bar = 2.0 * new_primal - primal
        flow_bar = 2.0 * new_flows - flows
        terms = jnp.dot(flow_bar, incidence, precision=highest)
        inflow_closing_output = lax.psum_scatter(terms, "region", scatter_dimension=1, tiled=True)
        image = jnp.dot(bar.reshape(-1, width), conversion, precision=highest).reshape(
            hours_dev, regions_dev, rows_bus
        )
        image = jnp.concatenate(
            [image[:, :, :1] + inflow_closing_output[:, :, None], image[:, :, 1:]], axis=2
        )
        prices = prices + sigma_step * (image - loads)
        levels_scale_run, levels_offset_run = lax.associative_scan(
            affine, (decay, bar[:, :, :units]), axis=0
        )
        carry_closing_output = carried_in(
            (levels_scale_run[-1], levels_offset_run[-1]), "tm", affine, identity, False
        )
        storage_dual = jnp.maximum(
            storage_dual
            + sigma_step
            * (
                level_scale * (levels_offset_run + levels_scale_run * carry_closing_output[1][None])
                - energy_cap[None]
            ),
            0.0,
        )
        partial_year = year_scale * jnp.sum(bar, axis=0)
        total = lax.psum(partial_year, "tm")
        year_dual = jnp.maximum(year_dual + sigma_step * (total - year_bound * annual_cap), 0.0)
        primal = new_primal
        flows = new_flows
    return (primal.astype(jnp.bfloat16), flows, prices, storage_dual, year_dual)


def solution(mesh):
    in_specs = (
        P("tm", "region", None),
        P("tm", "region", None),
        P(),
        P("region", None),
        P("tm", "region", None),
        P("region", None),
        P("region", None),
        P("region", None),
        P("region"),
    )
    out_specs = (
        P("tm", "region", None),
        P("tm", "region"),
        P("tm", "region", None),
        P("tm", "region", None),
        P("region", None),
    )
    return jax.shard_map(
        per_device, mesh=mesh, in_specs=in_specs, out_specs=out_specs, check_vma=False
    )
```

profile of v0, /device:TPU:0, one launch (start us, length us, event | category | flops | bytes accessed | tf_op | source)
XLA Modules:
  0.0 461.1 jit_solution(15444067455109021635)
XLA Ops:
  0.7 1.7 fusion.22
  2.4 2.0 fusion.8
  4.3 42.2 %all-reduce.45 = (f32[]{:T(128)}, f32[]{:T(128)}) all-reduce(f32[]{:T(128)} %fusion.8, f32[]{:T(128)} %fusion.22), channel_id=1, replica_groups=mesh['tm'=16,'region'=2] {'tm','region'}, use_global_device_ids=true, to_apply=%region_1.0 | all-reduce | flops 2 | bytes 16 | tf_op jit(solution)/shard_map/psum | solution.py:49
  47.9 0.8 slice_bitcast_fusion.1
  48.8 1.2 broadcast_multiply_fusion.2
  50.3 2.7 fusion
  53.6 2.8 collective-permute-start
  56.4 0.9 negate_select_fusion
  57.3 1.9 fusion.60
  59.2 0.7 slice.383
  59.9 0.7 slice.384
  60.6 1.0 multiply_add_fusion.2
  63.5 1.5 multiply_add_fusion.5
  65.0 1.4 slice.395
  66.4 1.4 slice.396
  67.8 1.4 slice.394
  69.2 1.4 slice.398
  70.6 1.4 slice.393
  72.0 1.4 slice.404
  73.4 1.4 slice.489
  74.8 1.4 slice.502
  78.7 0.7 slice.408
  80.0 0.8 multiply_add_fusion.8
  81.8 0.8 fusion.37
  82.6 0.7 pad_maximum_fusion.10
  84.2 0.7 pad_maximum_fusion.6
  85.3 40.3 %all_gather.20 = f32[16,12,128]{2,1,0:T(8,128)S(1)} all-gather(f32[1,12,128]{2,1,0:T(8,128)S(1)} %copy.31), channel_id=1, replica_groups=mesh['tm'=16,'region'=2] {'tm'}, dimensions={0}, use_global_device_ids=true | all-gather | bytes 104448 | tf_op jit(solution)/shard_map/all_gather | solution.py:18
  125.9 36.1 %all_gather.19 = f32[16,12,128]{2,1,0:T(8,128)S(1)} all-gather(f32[1,12,128]{2,1,0:T(8,128)S(1)} %copy.30), channel_id=1, replica_groups=mesh['tm'=16,'region'=2] {'tm'}, dimensions={0}, use_global_device_ids=true | all-gather | bytes 104448 | tf_op jit(solution)/shard_map/all_gather | solution.py:18
  162.7 0.7 multiply_multiply_fusion
  166.4 38.8 %all_gather.22 = f32[16,12,128]{2,1,0:T(8,128)S(1)} all-gather(f32[1,12,128]{2,1,0:T(8,128)S(1)} %copy.33), channel_id=1, replica_groups=mesh['tm'=16,'region'=2] {'tm'}, dimensions={0}, use_global_device_ids=true | all-gather | bytes 104448 | tf_op jit(solution)/shard_map/all_gather | solution.py:18
  205.2 36.1 %all_gather.21 = f32[16,12,128]{2,1,0:T(8,128)S(1)} all-gather(f32[1,12,128]{2,1,0:T(8,128)S(1)} %copy.32), channel_id=1, replica_groups=mesh['tm'=16,'region'=2] {'tm'}, dimensions={0}, use_global_device_ids=true | all-gather | bytes 104448 | tf_op jit(solution)/shard_map/all_gather | solution.py:18
  242.0 1.3 fusion.20
  243.4 73.7 %psum.30 = f32[12,1024]{1,0:T(8,128)S(1)} all-reduce(f32[12,1024]{1,0:T(8,128)S(1)} %broadcast_multiply_fusion.1), channel_id=1, replica_groups=mesh['tm'=16,'region'=2] {'tm'}, use_global_device_ids=true, to_apply=%region_10.11 | all-reduce | flops 12288 | bytes 98304 | tf_op jit(solution)/shard_map/psum | solution.py:118
  317.1 0.6 fusion.29
  317.8 0.7 maximum_add_fusion
  319.8 0.8 concatenate.96
  321.0 0.7 copy-done.25
  321.7 4.2 fusion.62
  326.8 0.7 slice.482
  328.1 1.1 fusion.17
  330.5 36.2 %all_gather.24 = f32[16,12,128]{2,1,0:T(8,128)S(1)} all-gather(f32[1,12,128]{2,1,0:T(8,128)S(1)} %copy.37), channel_id=1, replica_groups=mesh['tm'=16,'region'=2] {'tm'}, dimensions={0}, use_global_device_ids=true | all-gather | bytes 104448 | tf_op jit(solution)/shard_map/all_gather | solution.py:18
  366.7 84.2 %psum.31 = f32[12,1024]{1,0:T(8,128)S(1)} all-reduce(f32[12,1024]{1,0:T(8,128)S(1)} %broadcast_multiply_fusion), channel_id=1, replica_groups=mesh['tm'=16,'region'=2] {'tm'}, use_global_device_ids=true, to_apply=%region_15.16 | all-reduce | flops 12288 | bytes 98304 | tf_op jit(solution)/shard_map/psum | solution.py:118
  451.0 1.8 all-gather
  453.4 2.7 fusion.1
  456.1 2.2 collective-permute-start.1
  458.4 0.7 add_maximum_fusion
  459.1 0.7 add_maximum_fusion.1
  460.2 0.9 fusion.25
  (288 shorter events, 17.0 us)
Async XLA Ops:
  0.6 241.3 %copy-start = (f32[1024,256]{1,0:T(8,128)S(1)}, f32[1024,256]{1,0:T(8,128)}, u32[]{:S(2)}) copy-start(f32[1024,256]{1,0:T(8,128)} %param.17) | copy-start | bytes 3145732
  0.6 56.6 %copy-start.1 = (bf16[24,12,1024]{2,0,1:T(8,128)(2,1)S(1)}, bf16[24,12,1024]{2,0,1:T(8,128)(2,1)}, u32[]{:S(2)}) copy-start(bf16[24,12,1024]{2,0,1:T(8,128)(2,1)} %param.15) | copy-start | bytes 1769476
  48.7 1.3 copy-start.41
  48.7 7.7 %copy-start.43 = (s32[32]{0:T(128)}, s32[32]{0:T(128)S(1)}, u32[]{:S(2)}) copy-start(s32[32]{0:T(128)S(1)} %get-tuple-element.298) | copy-start | bytes 388
  53.0 3.4 copy-start.30
  53.6 266.3 %collective-permute-start = (f32[24,4]{0,1:T(4,128)}, f32[24,4]{0,1:T(4,128)}, u32[]{:S(2)}, u32[]{:S(2)}) collective-permute-start(f32[24,4]{0,1:T(4,128)} %slice.561), channel_id=1, source_target_pairs={{0,1},{2,3},{4,5},{6,7},{8,9},{10,11},{12,13},{14,15},{16,17},{18,... | collective-permute-start | bytes 1160
  57.3 1.9 copy-start.18
  57.3 3.2 copy-start.2
  62.8 20.9 %copy-start.11 = (f32[6,12,128]{2,0,1:T(8,128)}, f32[6,12,128]{2,0,1:T(8,128)S(1)}, u32[]{:S(2)}) copy-start(f32[6,12,128]{2,0,1:T(8,128)S(1)} %slice.388) | copy-start | bytes 110596
  78.7 5.1 %copy-start.13 = (f32[5,12,128]{2,0,1:T(8,128)S(1)}, f32[5,12,128]{2,0,1:T(8,128)}, u32[]{:S(2)}) copy-start(f32[5,12,128]{2,0,1:T(8,128)} %slice.387) | copy-start | bytes 92164
  78.7 5.1 %copy-start.24 = (f32[5,12,128]{2,0,1:T(8,128)S(1)}, f32[5,12,128]{2,0,1:T(8,128)}, u32[]{:S(2)}) copy-start(f32[5,12,128]{2,0,1:T(8,128)} %slice.406) | copy-start | bytes 92164
  79.4 5.6 %copy-start.6 = (f32[11,12,128]{2,0,1:T(8,128)}, f32[11,12,128]{2,0,1:T(8,128)S(1)}, u32[]{:S(2)}) copy-start(f32[11,12,128]{2,0,1:T(8,128)S(1)} %slice.380) | copy-start | bytes 202756
  80.0 3.8 copy-start.36
  83.3 1.7 copy-start.14
  83.8 1.3 copy-start.34
  85.1 77.6 %copy-start.32 = (f32[12,128]{1,0:T(8,128)S(1)}, f32[12,128]{1,0:T(8,128)}, u32[]{:S(2)}) copy-start(f32[12,128]{1,0:T(8,128)} %param.20) | copy-start | bytes 18436
  162.1 0.6 copy-start.16
  166.1 75.9 %copy-start.17 = (f32[12,1024]{1,0:T(8,128)S(1)}, f32[12,1024]{1,0:T(8,128)}, u32[]{:S(2)}) copy-start(f32[12,1024]{1,0:T(8,128)} %param.18) | copy-start | bytes 147460
  166.1 75.9 %copy-start.19 = (f32[12,1024]{1,0:T(8,128)S(1)}, f32[12,1024]{1,0:T(8,128)}, u32[]{:S(2)}) copy-start(f32[12,1024]{1,0:T(8,128)} %copy-done.18) | copy-start | bytes 147460
  241.9 1.4 copy-start.20
  242.0 75.1 %copy-start.21 = (f32[12,1024]{1,0:T(8,128)S(1)}, f32[12,1024]{1,0:T(8,128)}, u32[]{:S(2)}) copy-start(f32[12,1024]{1,0:T(8,128)} %param.21) | copy-start | bytes 147460
  243.3 75.1 %copy-start.40 = (u32[32]{0:T(128)S(1)}, u32[32]{0:T(128)}, u32[]{:S(2)}) copy-start(u32[32]{0:T(128)} %constant.173) | copy-start | bytes 388
  243.4 76.5 %copy-start.31 = (f32[24,16]{0,1:T(8,128)S(1)}, f32[24,16]{0,1:T(8,128)}, u32[]{:S(2)}) copy-start(f32[24,16]{0,1:T(8,128)} %copy-done.30) | copy-start | bytes 4612
  317.0 3.6 copy-start.9
  317.0 3.8 copy-start.5
  320.8 0.9 copy-start.25
  321.7 7.5 %copy-start.3 = (f32[24,12,256]{2,0,1:T(8,128)}, f32[24,12,256]{2,0,1:T(8,128)S(1)}, u32[]{:S(2)}) copy-start(f32[24,12,256]{2,0,1:T(8,128)S(1)} %fusion.23) | copy-start | bytes 884740
  325.9 0.8 copy-start.12
  328.1 1.2 copy-start.23
  328.1 1.2 copy-start.27
  328.1 1.4 copy-start.28
  329.2 0.9 copy-start.7
  329.2 0.9 copy-start.15
  329.2 1.1 copy-start.35
  329.8 36.8 %copy-start.29 = (f32[12,1024]{1,0:T(8,128)S(1)}, f32[12,1024]{1,0:T(8,128)}, u32[]{:S(2)}) copy-start(f32[12,1024]{1,0:T(8,128)} %get-tuple-element.242) | copy-start | bytes 147460
  330.0 120.9 %slice-start = ((f32[24,12,256]{2,0,1:T(8,128)}), f32[24,12,1]{2,0,1:T(8,128)S(1)}, s32[]{:S(2)}) async-start(f32[24,12,256]{2,0,1:T(8,128)} %copy-done.3), calls=%async_computation | async-start | bytes 294912 | tf_op jit(solution)/shard_map/slice | solution.py:87
  330.1 122.8 %copy-start.37 = (f32[32]{0:T(128)S(1)}, f32[32]{0:T(128)}, u32[]{:S(2)}) copy-start(f32[32]{0:T(128)} %param.23) | copy-start | bytes 388
  330.1 122.7 %copy-start.38 = (f32[32]{0:T(128)S(1)}, f32[32]{0:T(128)}, u32[]{:S(2)}) copy-start(f32[32]{0:T(128)} %get-tuple-element.258) | copy-start | bytes 388
  330.1 122.7 %copy-start.39 = (f32[32]{0:T(128)S(1)}, f32[32]{0:T(128)}, u32[]{:S(2)}) copy-start(f32[32]{0:T(128)} %get-tuple-element.299) | copy-start | bytes 388
  330.1 122.7 %copy-start.42 = (s32[32]{0:T(128)S(1)}, s32[32]{0:T(128)}, u32[]{:S(2)}) copy-start(s32[32]{0:T(128)} %copy-done.41) | copy-start | bytes 388
  330.1 122.7 %copy-start.44 = (s32[32]{0:T(128)S(1)}, s32[32]{0:T(128)}, u32[]{:S(2)}) copy-start(s32[32]{0:T(128)} %copy-done.43) | copy-start | bytes 388
  330.2 128.2 %copy-start.8 = (f32[24,12,128]{2,0,1:T(8,128)S(1)}, f32[24,12,128]{2,0,1:T(8,128)}, u32[]{:S(2)}) copy-start(f32[24,12,128]{2,0,1:T(8,128)} %get-tuple-element.250) | copy-start | bytes 442372
  330.2 128.2 %copy-start.33 = (f32[12,128]{1,0:T(8,128)S(1)}, f32[12,128]{1,0:T(8,128)}, u32[]{:S(2)}) copy-start(f32[12,128]{1,0:T(8,128)} %param.20) | copy-start | bytes 18436
  330.3 128.7 %copy-start.10 = (f32[12,1024]{1,0:T(8,128)S(1)}, f32[12,1024]{1,0:T(8,128)}, u32[]{:S(2)}) copy-start(f32[12,1024]{1,0:T(8,128)} %copy-done.9) | copy-start | bytes 147460
  330.3 128.7 %copy-start.22 = (f32[12,1024]{1,0:T(8,128)S(1)}, f32[12,1024]{1,0:T(8,128)}, u32[]{:S(2)}) copy-start(f32[12,1024]{1,0:T(8,128)} %param.21) | copy-start | bytes 147460
  453.1 7.1 %copy-start.45 = (f32[24,32]{1,0:T(8,128)}, f32[24,32]{1,0:T(8,128)S(1)}, u32[]{:S(2)}) copy-start(f32[24,32]{1,0:T(8,128)S(1)} %fusion.16) | copy-start | bytes 9220
  453.1 7.1 %copy-start.4 = (f32[24,12,256]{2,0,1:T(8,128)S(1)}, f32[24,12,256]{2,0,1:T(8,128)}, u32[]{:S(2)}) copy-start(f32[24,12,256]{2,0,1:T(8,128)} %copy-done.3) | copy-start | bytes 884740
  456.1 3.8 collective-permute-start.1
  (1 other events, 0.6 us)
where the time goes:
time: 463 us; the launch traced here: 461 us
  blocking collectives  395 us (85%)
  local copies, waits for them, and re-layouts  30.4 us (7%)
  other arithmetic  18.7 us (4%)
  matrix products  7.4 us (2%)
  starting transfers between devices  5.06 us (1%)
    all_gather x5, blocking collectives, carried_in(): gathered = jax.tree.map(lambda a: lax.all_gather(a, axis), part)  188 us
    psum x2, blocking collectives, per_device(): total = lax.psum(partial_year, 'tm')  158 us
    psum x1, blocking collectives, per_device(): lax.psum((jnp.sum(costs * costs), jnp.sum(loads * loads)), ('tm', 'region'))  42.2 us
    slice x36, local copies, waits for them, and re-layouts, per_device(): lax.associative_scan(affine, (decay, bar[:, :, :units]), axis=0)  19.8 us
  transfers between devices with their start and end apart: 2, of which 0 were waited for; matrix products, arithmetic and copies ran while one was open for 8% of the time, Pallas kernels for 0%

commit v1 on v0

v1 whole, which is shorter than its diff:
```python
import functools
import math

import jax
import jax.numpy as jnp
from jax import lax
from jax.experimental import pallas as pl
from jax.experimental.pallas import tpu as pltpu
from jax.sharding import PartitionSpec as P

step_ratio = 0.5
LANES = 128
SUBLANES = 8
CHUNK = 256


def up_to(value, multiple):
    return -(-value // multiple) * multiple


def padded(x, rows):
    missing = rows - x.shape[0]
    if missing == 0:
        return x
    return jnp.concatenate([x, jnp.zeros((missing,) + x.shape[1:], x.dtype)], axis=0)


def split_in_two(x):
    high = x.astype(jnp.bfloat16)
    return high, (x - high.astype(jnp.float32)).astype(jnp.bfloat16)


def product(a_high, a_low, b_high, b_low, contract_b):
    dims = (((1,), (contract_b,)), ((), ()))
    dot = functools.partial(
        lax.dot_general, dimension_numbers=dims, preferred_element_type=jnp.float32
    )
    return dot(a_high, b_high) + (dot(a_high, b_low) + dot(a_low, b_high))


def kernel(
    time_count,
    group_count,
    cost,
    demand,
    conversion,
    upper,
    decay,
    energy_cap,
    annual_cap,
    line_ends,
    line_cap,
    primal_out,
    flows_out,
    prices_out,
    storage_out,
    year_out,
    conv_high,
    conv_low,
    bar_high,
    bar_low,
    price_high,
    price_low,
    prices,
    image,
    back,
    keep,
    charge,
    levels,
    storage,
    stored,
    lower,
    year_sum,
    year_dual,
    square_recv,
    bus_recv,
    inflow_recv,
    first_send,
    first_recv,
    spread_send,
    spread_recv,
    turn_send,
    turn_recv,
    again_send,
    again_recv,
    last_send,
    last_recv,
    send_sem,
    recv_sem,
    group_send_sem,
    group_recv_sem,
):
    me = lax.axis_index("tm")
    group = lax.axis_index("region")
    regions, hours, width = cost.shape
    rows_bus = demand.shape[2]
    units = decay.shape[1]
    rows = lower.shape[0]
    pair = (2 * SUBLANES) // math.gcd(hours, 2 * SUBLANES)
    chunks = [slice(i, i + CHUNK) for i in range(0, width, CHUNK)]
    blocks = width // LANES
    tiles = (rows // SUBLANES) * blocks
    share = -(-tiles // time_count)
    hours_all = hours * time_count
    scale = 1.0 / math.sqrt(hours_all)
    year_bound = math.sqrt(hours_all)
    f32 = jnp.float32

    barrier = pltpu.get_barrier_semaphore()

    def greet_time(k, _):
        pl.semaphore_signal(
            barrier,
            inc=1,
            device_id={"tm": lax.rem(me + k, time_count)},
            device_id_type=pl.DeviceIdType.MESH,
        )
        return 0

    lax.fori_loop(1, time_count, greet_time, 0)

    def greet_group(k, _):
        pl.semaphore_signal(
            barrier,
            inc=1,
            device_id={"region": lax.rem(group + k, group_count)},
            device_id_type=pl.DeviceIdType.MESH,
        )
        return 0

    lax.fori_loop(1, group_count, greet_group, 0)

    def send_time(phase, source_of, recv):
        def one(k, _):
            peer = lax.rem(me + k, time_count)
            pltpu.make_async_remote_copy(
                src_ref=source_of(peer),
                dst_ref=recv.at[me],
                send_sem=send_sem.at[phase],
                recv_sem=recv_sem.at[phase],
                device_id={"tm": peer},
                device_id_type=pl.DeviceIdType.MESH,
            ).start()
            return 0

        lax.fori_loop(1, time_count, one, 0)

    def send_group(phase, recv):
        def one(k, _):
            pltpu.make_async_remote_copy(
                src_ref=recv.at[group],
                dst_ref=recv.at[group],
                send_sem=group_send_sem.at[phase],
                recv_sem=group_recv_sem.at[phase],
                device_id={"region": lax.rem(group + k, group_count)},
                device_id_type=pl.DeviceIdType.MESH,
            ).start()
            return 0

        lax.fori_loop(1, group_count, one, 0)

    def await_bytes(recv, count, sem):
        if count > 1:
            part = recv.at[pl.ds(0, count - 1)]
            pltpu.make_async_copy(part, part, sem).wait()

    zero_units = jnp.zeros((regions, units), f32)
    for t in range(hours):
        keep[t] = decay[pl.ds(t, regions, stride=hours), :]

    def square_sums(r, carry):
        a, b = carry
        for chunk in chunks:
            c = cost[r, :, chunk].astype(f32)
            a = a + c * c
        l = demand[r].astype(f32)
        return a, b + l * l

    a, b = lax.fori_loop(
        0,
        regions,
        square_sums,
        (jnp.zeros((hours, CHUNK), f32), jnp.zeros((hours, rows_bus), f32)),
    )
    whole_decay = lax.fori_loop(
        0, hours, lambda t, d: d * keep[t], jnp.ones((regions, units), f32)
    )

    def folded(x):
        x = jnp.sum(x, axis=0, keepdims=True)
        return sum(x[:, i * LANES : (i + 1) * LANES] for i in range(x.shape[1] // LANES))

    own_squares = padded(jnp.concatenate([folded(a), folded(b)], axis=0), SUBLANES)
    square_recv[group] = own_squares
    pl.semaphore_wait(barrier, time_count - 1 + group_count - 1)
    send_group(0, square_recv)
    column = lax.broadcasted_iota(jnp.int32, (regions, width), 1)
    lower[0:regions, :] = jnp.where(column < units, -upper[...], 0.0)
    year_sum[...] = jnp.zeros_like(year_sum)
    conv = conversion[...]
    high, low = split_in_two(conv)
    conv_high[...] = high
    conv_low[...] = low
    await_bytes(square_recv, group_count, group_recv_sem.at[0])
    squares = jnp.sum(square_recv[...], axis=0)
    first_send[0:rows, :] = padded(whole_decay, rows)
    first_send[rows : rows + SUBLANES, :] = squares
    first_recv[me, 0:rows, :] = padded(whole_decay, rows)
    first_recv[me, rows : rows + SUBLANES, :] = squares
    send_time(0, lambda peer: first_send, first_recv)

    bus_width = bus_recv.shape[2]
    ends = line_ends[...]
    region_id = lax.broadcasted_iota(jnp.int32, (bus_width, ends.shape[1]), 0)
    incidence = (ends[1:2, :] == region_id).astype(f32) - (ends[0:1, :] == region_id).astype(f32)
    spot = lax.broadcasted_iota(jnp.int32, (hours, bus_width), 1) - group * regions

    await_bytes(first_recv, time_count, recv_sem.at[0])
    squares = jnp.sum(first_recv[:, rows : rows + SUBLANES, :], axis=0)
    sums = jnp.sum(squares, axis=1, keepdims=True)
    omega = jnp.sqrt(sums[0:1] / sums[1:2])
    tau = step_ratio / omega
    sigma = step_ratio * omega

    def hours_of(r):
        return pl.ds(pl.multiple_of(r * hours, SUBLANES), hours)

    def over_regions(one):
        def several(i, _):
            first = i * pair
            together = pl.ds(pl.multiple_of(first * hours, 2 * SUBLANES), pair * hours)
            for chunk in chunks:
                bars = [one(first + j, chunk) for j in range(pair)]
                high, low = split_in_two(jnp.concatenate(bars, axis=0))
                bar_high[together, chunk] = high
                bar_low[together, chunk] = low
            return 0

        lax.fori_loop(0, regions // pair, several, 0)

    def keep_sums(r, chunk, bar):
        year_sum[pl.ds(r, 1), chunk] = jnp.sum(bar, axis=0, keepdims=True)
        if chunk.start < units:
            charge[hours_of(r), :] = bar[:, :units]

    def first_primal(r, chunk):
        c = cost[r, :, chunk].astype(f32)
        low, high = lower[pl.ds(r, 1), chunk], upper[pl.ds(r, 1), chunk]
        return c, low, high, jnp.clip(-tau * c, low, high)

    def first_pass(r, chunk):
        bar = 2.0 * first_primal(r, chunk)[3]
        keep_sums(r, chunk, bar)
        return bar

    over_regions(first_pass)

    def send_sums(phase, send, recv):
        def run_levels(t, level):
            level = keep[t] * level + charge[pl.ds(t, regions, stride=hours), :]
            levels[t] = level
            return level

        level = padded(lax.fori_loop(0, hours, run_levels, zero_units, unroll=4), rows)
        for owner in range(time_count):
            send[owner, 0:rows, :] = level
            for j in range(share):
                tile = owner * share + j
                if tile < tiles:
                    half, block = tile // blocks, tile % blocks
                    part = year_sum[
                        half * SUBLANES : (half + 1) * SUBLANES,
                        block * LANES : (block + 1) * LANES,
                    ]
                else:
                    part = jnp.zeros((SUBLANES, LANES), f32)
                at = rows + j * SUBLANES
                send[owner, at : at + SUBLANES, :] = part
        recv[me] = send[me]
        send_time(phase, lambda peer: send.at[peer], recv)

    def matmul_image():
        image[...] = product(bar_high[...], bar_low[...], conv_high[...], conv_low[...], 0)

    send_sums(1, spread_send, spread_recv)
    matmul_image()

    def first_prices(i, bus):
        first = i * pair
        together = pl.ds(pl.multiple_of(first * hours, 2 * SUBLANES), pair * hours)
        parts = []
        for j in range(pair):
            r = first + j
            p = sigma * (image[hours_of(r), :] - demand[r].astype(f32))
            prices[hours_of(r), :] = p
            bus = jnp.where(spot == r, p[:, 0:1], bus)
            parts.append(p)
        high, low = split_in_two(jnp.concatenate(parts, axis=0))
        price_high[together, :] = high
        price_low[together, :] = low
        return bus

    bus_recv[group] = lax.fori_loop(
        0, regions // pair, first_prices, jnp.zeros((hours, bus_width), f32)
    )
    send_group(1, bus_recv)
    back[...] = product(price_high[...], price_low[...], conv_high[...], conv_low[...], 1)

    await_bytes(spread_recv, time_count, recv_sem.at[1])

    def carried(recv):
        def one(j, state):
            return first_recv[j, 0:rows, :] * state + recv[j, 0:rows, :]

        state = lax.fori_loop(0, me, one, jnp.zeros((rows, units), f32))
        return state[0:regions]

    def year_total(recv):
        return jnp.sum(recv[:, rows:, :], axis=0)

    own_year = year_total(spread_recv)
    turn = carried(spread_recv)
    caps = energy_cap[...]

    def first_storage(t, run):
        run = keep[t] * run
        dual = jnp.maximum(sigma * (scale * (levels[t] + run) - caps), 0.0)
        storage[t] = dual
        return run

    lax.fori_loop(0, hours, first_storage, turn, unroll=4)

    def adjoint_only(i, run):
        t = hours - 1 - i
        return keep[t] * (scale * storage[t] + run)

    run = lax.fori_loop(0, hours, adjoint_only, zero_units, unroll=4)
    turn_send[0:rows, :] = padded(run, rows)
    turn_send[rows:, :] = own_year
    turn_recv[me, 0:rows, :] = padded(run, rows)
    turn_recv[me, rows:, :] = own_year
    send_time(2, lambda peer: turn_send, turn_recv)

    await_bytes(bus_recv, group_count, group_recv_sem.at[1])
    exact = functools.partial(
        lax.dot_general, precision=lax.Precision.HIGHEST, preferred_element_type=f32
    )
    bus = jnp.sum(bus_recv[...], axis=0)
    flow_grad = exact(bus, incidence, (((1,), (0,)), ((), ())))
    caps_of_lines = line_cap[...]
    flows = jnp.clip(-tau * flow_grad, -caps_of_lines, caps_of_lines)
    flows_out[...] = flows
    inflow_recv[group] = exact(2.0 * flows, incidence, (((1,), (1,)), ((), ())))
    send_group(2, inflow_recv)

    await_bytes(turn_recv, time_count, recv_sem.at[2])

    def ahead(i, state):
        j = time_count - 1 - i
        return first_recv[j, 0:rows, :] * state + turn_recv[j, 0:rows, :]

    run = lax.fori_loop(0, time_count - 1 - me, ahead, jnp.zeros((rows, units), f32))[0:regions]

    def adjoint(i, run):
        t = hours - 1 - i
        value = scale * storage[t] + run
        stored[pl.ds(t, regions, stride=hours), :] = value
        return keep[t] * value

    lax.fori_loop(0, hours, adjoint, run, unroll=4)

    def year_parts(recv_tile):
        for tile in range(tiles):
            half, block = tile // blocks, tile % blocks
            first = half * SUBLANES
            last = min(first + SUBLANES, regions)
            if last <= first:
                continue
            at = rows + (tile % share) * SUBLANES
            total = recv_tile(tile // share, at)[0 : last - first]
            cap = annual_cap[first:last, block * LANES : (block + 1) * LANES]
            step = sigma * (scale * total - year_bound * cap)
            yield slice(first, last), slice(block * LANES, (block + 1) * LANES), step

    for r, c, step in year_parts(lambda owner, at: turn_recv[owner, at : at + SUBLANES, :]):
        year_dual[r, c] = jnp.maximum(step, 0.0)

    def second_pass(r, chunk):
        c, low, high, x = first_primal(r, chunk)
        grad = c + back[hours_of(r), chunk] + scale * year_dual[pl.ds(r, 1), chunk]
        if chunk.start < units:
            grad = jnp.concatenate(
                [grad[:, :units] + stored[hours_of(r), :], grad[:, units:]], axis=1
            )
        new = jnp.clip(x - tau * grad, low, high)
        primal_out[r, :, chunk] = new.astype(jnp.bfloat16)
        bar = 2.0 * new - x
        keep_sums(r, chunk, bar)
        return bar

    over_regions(second_pass)
    send_sums(3, again_send, again_recv)
    matmul_image()
    await_bytes(inflow_recv, group_count, group_recv_sem.at[2])
    inflow = jnp.sum(inflow_recv[...], axis=0)
    bus_row = lax.broadcasted_iota(jnp.int32, (hours, rows_bus), 1) == 0

    def second_prices(r, _):
        load = demand[r].astype(f32)
        into = jnp.sum(jnp.where(spot == r, inflow, 0.0), axis=1, keepdims=True)
        whole = image[hours_of(r), :] + jnp.where(bus_row, into, 0.0)
        prices_out[r] = prices[hours_of(r), :] + sigma * (whole - load)
        return 0

    lax.fori_loop(0, regions, second_prices, 0)

    await_bytes(again_recv, time_count, recv_sem.at[3])
    own_year = year_total(again_recv)
    last_send[...] = own_year
    last_recv[me] = own_year
    send_time(4, lambda peer: last_send, last_recv)
    turn = carried(again_recv)

    def second_storage(t, run):
        run = keep[t] * run
        storage_out[pl.ds(t, regions, stride=hours), :] = jnp.maximum(
            storage[t] + sigma * (scale * (levels[t] + run) - caps), 0.0
        )
        return run

    lax.fori_loop(0, hours, second_storage, turn, unroll=4)
    await_bytes(last_recv, time_count, recv_sem.at[4])
    for r, c, step in year_parts(
        lambda owner, at: last_recv[owner, at - rows : at - rows + SUBLANES, :]
    ):
        year_out[r, c] = jnp.maximum(year_dual[r, c] + step, 0.0)

    for phase, recv in enumerate((first_recv, spread_recv, turn_recv, again_recv, last_recv)):
        await_bytes(recv, time_count, send_sem.at[phase])
    for phase, recv in enumerate((square_recv, bus_recv, inflow_recv)):
        await_bytes(recv, group_count, group_send_sem.at[phase])


def deliver(*refs):
    count = (len(refs) - 1) // 2
    sem = refs[-1]
    copies = [
        pltpu.make_async_copy(refs[i], refs[count + i], sem.at[i]) for i in range(count)
    ]
    for copy in copies:
        copy.start()
    for copy in copies:
        copy.wait()


def delivered(arrays):
    return pl.pallas_call(
        deliver,
        out_shape=tuple(jax.ShapeDtypeStruct(a.shape, a.dtype) for a in arrays),
        in_specs=[pl.BlockSpec(memory_space=pltpu.VMEM)] * len(arrays),
        out_specs=[pl.BlockSpec(memory_space=pl.ANY)] * len(arrays),
        scratch_shapes=[pltpu.SemaphoreType.DMA((len(arrays),))],
        compiler_params=pltpu.CompilerParams(vmem_limit_bytes=8 * 2**20),
    )(*arrays)


def per_device(
    time_count,
    group_count,
    cost,
    demand,
    conversion,
    upper,
    decay,
    energy_cap,
    annual_cap,
    line_ends,
    line_cap,
):
    f32, bf16 = jnp.float32, jnp.bfloat16
    hours, regions, width = cost.shape
    rows_bus = demand.shape[2]
    units = decay.shape[2]
    lines = line_ends.shape[0]
    rows = up_to(regions, 2 * SUBLANES)
    bus_width = up_to(regions * group_count, LANES)
    tiles = (rows // SUBLANES) * (width // LANES)
    share = -(-tiles // time_count) * SUBLANES
    vmem = pl.BlockSpec(memory_space=pltpu.VMEM)
    scratch = lambda *shape: pltpu.VMEM(shape, f32)
    half = lambda *shape: pltpu.VMEM(shape, bf16)
    flat = hours * regions
    by_region = lambda x: jnp.transpose(x, (1, 0, 2))
    results = pl.pallas_call(
        functools.partial(kernel, time_count, group_count),
        out_shape=(
            jax.ShapeDtypeStruct((regions, hours, width), bf16),
            jax.ShapeDtypeStruct((hours, lines), f32),
            jax.ShapeDtypeStruct((regions, hours, rows_bus), f32),
            jax.ShapeDtypeStruct((flat, units), f32),
            jax.ShapeDtypeStruct((regions, width), f32),
        ),
        in_specs=[vmem] * 9,
        out_specs=[vmem] * 5,
        scratch_shapes=[
            half(width, rows_bus),
            half(width, rows_bus),
            half(flat, width),
            half(flat, width),
            half(flat, rows_bus),
            half(flat, rows_bus),
            scratch(flat, rows_bus),
            scratch(flat, rows_bus),
            scratch(flat, width),
            scratch(hours, regions, units),
            scratch(flat, units),
            scratch(hours, regions, units),
            scratch(hours, regions, units),
            scratch(flat, units),
            scratch(rows, width),
            scratch(rows, width),
            scratch(rows, width),
            scratch(group_count, SUBLANES, LANES),
            scratch(group_count, hours, bus_width),
            scratch(group_count, hours, bus_width),
            scratch(rows + SUBLANES, units),
            scratch(time_count, rows + SUBLANES, units),
            scratch(time_count, rows + share, units),
            scratch(time_count, rows + share, units),
            scratch(rows + share, units),
            scratch(time_count, rows + share, units),
            scratch(time_count, rows + share, units),
            scratch(time_count, rows + share, units),
            scratch(share, units),
            scratch(time_count, share, units),
            pltpu.SemaphoreType.DMA((5,)),
            pltpu.SemaphoreType.DMA((5,)),
            pltpu.SemaphoreType.DMA((3,)),
            pltpu.SemaphoreType.DMA((3,)),
        ],
        compiler_params=pltpu.CompilerParams(
            collective_id=0, has_side_effects=True, vmem_limit_bytes=20 * 2**20
        ),
    )(
        by_region(cost),
        by_region(demand),
        conversion,
        upper,
        by_region(decay).reshape(flat, units),
        energy_cap,
        annual_cap,
        line_ends.T,
        line_cap.reshape(1, lines),
    )
    primal, flows, prices, storage, year = delivered(results)
    return (
        by_region(primal),
        flows,
        by_region(prices),
        by_region(storage.reshape(regions, hours, units)),
        year,
    )


def solution(mesh):
    in_specs = (
        P("tm", "region", None),
        P("tm", "region", None),
        P(),
        P("region", None),
        P("tm", "region", None),
        P("region", None),
        P("region", None),
        P("region", None),
        P("region"),
    )
    out_specs = (
        P("tm", "region", None),
        P("tm", "region"),
        P("tm", "region", None),
        P("tm", "region", None),
        P("region", None),
    )
    return jax.shard_map(
        functools.partial(per_device, mesh.shape["tm"], mesh.shape["region"]),
        mesh=mesh,
        in_specs=in_specs,
        out_specs=out_specs,
        check_vma=False,
    )
```

time: 463 us -> 48.1 us (0.10)
  blocking collectives: 395 us -> 0 us
  Pallas kernels: 0 us -> 40 us
  local copies, waits for them, and re-layouts: 30.4 us -> 7.12 us
  other arithmetic: 18.7 us -> 0 us
  matrix products: 7.4 us -> 0 us
  starting transfers between devices: 5.06 us -> 0 us
    psum x3 -> x0, blocking collectives: 200 us -> none  [the longest x2 158 us: per_device(): total = lax.psum(partial_year, 'tm')]
    all_gather x6 -> x0, blocking collectives: 189 us -> none  [the longest x5 188 us: carried_in(): gathered = jax.tree.map(lambda a: lax.all_gather(a, axis), part)]
    pallas_call x0 -> x2, Pallas kernels: none -> 40 us  [the longest x1 38.9 us: per_device(): pl.pallas_call(functools.partial(kernel, time_count, group_count), out_sh...]
    slice x75 -> x0, local copies, waits for them, and re-layouts: 20.8 us -> none  [the longest x36 19.8 us: per_device(): lax.associative_scan(affine, (decay, bar[:, :, :units]), axis=0)]
    dot_general x6 -> x0, matrix products: 7.4 us -> none  [the longest x1 4.17 us: per_device(): jnp.dot(prices.reshape(-1, rows_bus), conversion.T, precision=highest)]
    add x62 -> x0, other arithmetic: 6.5 us -> none  [the longest x36 4.59 us: affine(): return (earlier[0] * later[0], later[0] * earlier[1] + later[1])]
    reduce_sum x3 -> x0, other arithmetic: 5.56 us -> none  [the longest x1 1.97 us: per_device(): jnp.sum(costs * costs)]
    unnamed x2 -> x0, blocking collectives: 5.34 us -> none
  transfers between devices with their start and end apart: 2 -> 0, of which waited for: 0 -> 0; matrix products, arithmetic and copies ran while one was open for 8% -> 0% of each run, Pallas kernels for 0% -> 0%
where the time goes in v1:
time: 48.1 us; the launch traced here: 47.8 us
  Pallas kernels  40 us (83%)
  local copies, waits for them, and re-layouts  7.12 us (15%)
  between operations  0.67 us (1%)
    pallas_call x1, Pallas kernels, per_device(): pl.pallas_call(functools.partial(kernel, time_count, group_count), out_sh...  38.9 us
    unnamed x18, local copies, waits for them, and re-layouts  7.12 us
    pallas_call x1, Pallas kernels, delivered(): pl.pallas_call(deliver, out_shape=tuple((jax.ShapeDtypeStruct(a.shape, a....  1.02 us

profile of v1, /device:TPU:0, one launch (start us, length us, event | category | flops | bytes accessed | tf_op | source)
XLA Modules:
  0.0 47.8 jit_solution(4127842226109718265)
XLA Ops:
  0.6 0.0 copy-start.6
  0.6 0.0 copy-start.7
  0.7 0.7 %copy-done.6 = f32[12,128]{1,0:T(8,128)S(1)} copy-done((f32[12,128]{1,0:T(8,128)S(1)}, f32[12,128]{1,0:T(8,128)}, u32[]{:S(2)}) %copy-start.6) | copy-done | bytes 6168
  1.3 0.0 copy-done.7
  1.3 0.0 copy-start
  1.3 1.2 %copy-done = f32[1024,256]{1,0:T(8,128)S(1)} copy-done((f32[1024,256]{1,0:T(8,128)S(1)}, f32[1024,256]{1,0:T(8,128)}, u32[]{:S(2)}) %copy-start) | copy-done | bytes 1048600
  2.6 0.0 copy-start.1
  2.6 1.1 %copy-done.1 = bf16[24,12,1024]{2,0,1:T(8,128)(2,1)S(1)} copy-done((bf16[24,12,1024]{2,0,1:T(8,128)(2,1)S(1)}, bf16[24,12,1024]{2,0,1:T(8,128)(2,1)}, u32[]{:S(2)}) %copy-start.1) | copy-done | bytes 589848
  3.6 0.0 copy-start.2
  3.6 0.9 %copy-done.2 = bf16[24,12,256]{2,0,1:T(8,128)(2,1)S(1)} copy-done((bf16[24,12,256]{2,0,1:T(8,128)(2,1)S(1)}, bf16[24,12,256]{2,0,1:T(8,128)(2,1)}, u32[]{:S(2)}) %copy-start.2) | copy-done | bytes 147480
  4.5 0.0 copy-start.3
  4.5 0.9 %copy-done.3 = f32[24,12,128]{2,0,1:T(8,128)S(1)} copy-done((f32[24,12,128]{2,0,1:T(8,128)S(1)}, f32[24,12,128]{2,0,1:T(8,128)}, u32[]{:S(2)}) %copy-start.3) | copy-done | bytes 147480
  5.4 0.0 copy-start.4
  5.4 0.8 %copy-done.4 = f32[12,1024]{1,0:T(8,128)S(1)} copy-done((f32[12,1024]{1,0:T(8,128)S(1)}, f32[12,1024]{1,0:T(8,128)}, u32[]{:S(2)}) %copy-start.4) | copy-done | bytes 49176
  6.3 0.0 copy-start.5
  6.3 0.8 %copy-done.5 = f32[12,1024]{1,0:T(8,128)S(1)} copy-done((f32[12,1024]{1,0:T(8,128)S(1)}, f32[12,1024]{1,0:T(8,128)}, u32[]{:S(2)}) %copy-start.5) | copy-done | bytes 49176
  7.1 0.0 copy-start.8
  7.1 0.7 %copy-done.8 = f32[32]{0:T(128)S(1)} copy-done((f32[32]{0:T(128)S(1)}, f32[32]{0:T(128)}, u32[]{:S(2)}) %copy-start.8) | copy-done | bytes 152
  7.8 38.9 %shard_map.128 = (bf16[12,24,1024]{2,1,0:T(8,128)(2,1)S(1)}, f32[24,32]{1,0:T(8,128)S(1)}, f32[12,24,256]{2,1,0:T(8,128)S(1)}, f32[288,128]{1,0:T(8,128)S(1)}, f32[12,1024]{1,0:T(8,128)S(1)}) custom-call(bf16[12,24,1024]{2,1,0:T(8,128)(2,1)S(1)} %bitcast.12, bf16[12,24,256]{2,1,0:T(8,128)(2,1)S(1)} %bitcast.13, f32[1024,256]{1,0:T(8,128)S(1)} %copy-done, ...), custom_call_target="tpu_custom_call" | custom-call | tf_op jit(solution)/shard_map/pallas_call | solution.py:494
  46.7 1.0 %shard_map.129 = (bf16[12,24,1024]{2,1,0:T(8,128)(2,1)}, f32[24,32]{1,0:T(8,128)}, f32[12,24,256]{2,1,0:T(8,128)}, f32[288,128]{1,0:T(8,128)}, f32[12,1024]{1,0:T(8,128)}) custom-call(bf16[12,24,1024]{2,1,0:T(8,128)(2,1)S(1)} %get-tuple-element.15.refs_0_, f32[24,32]{1,0:T(8,128)S(1)} %get-tuple-element.16.refs_1_, ...), custom_call_target="tpu_custom_call" | custom-call | tf_op jit(solution)/shard_map/pallas_call | solution.py:457
Async XLA Ops:
  0.6 0.7 %copy-start.6 = (f32[12,128]{1,0:T(8,128)S(1)}, f32[12,128]{1,0:T(8,128)}, u32[]{:S(2)}) copy-start(f32[12,128]{1,0:T(8,128)} %energy_cap.1) | copy-start | bytes 18436
  0.6 0.7 %copy-start.7 = (s32[32,2]{0,1:T(2,128)S(1)}, s32[32,2]{0,1:T(2,128)}, u32[]{:S(2)}) copy-start(s32[32,2]{0,1:T(2,128)} %param.16) | copy-start | bytes 772
  1.3 1.2 %copy-start = (f32[1024,256]{1,0:T(8,128)S(1)}, f32[1024,256]{1,0:T(8,128)}, u32[]{:S(2)}) copy-start(f32[1024,256]{1,0:T(8,128)} %conversion.1) | copy-start | bytes 3145732
  2.6 1.1 %copy-start.1 = (bf16[24,12,1024]{2,0,1:T(8,128)(2,1)S(1)}, bf16[24,12,1024]{2,0,1:T(8,128)(2,1)}, u32[]{:S(2)}) copy-start(bf16[24,12,1024]{2,0,1:T(8,128)(2,1)} %param.9) | copy-start | bytes 1769476
  3.6 0.9 %copy-start.2 = (bf16[24,12,256]{2,0,1:T(8,128)(2,1)S(1)}, bf16[24,12,256]{2,0,1:T(8,128)(2,1)}, u32[]{:S(2)}) copy-start(bf16[24,12,256]{2,0,1:T(8,128)(2,1)} %param.10) | copy-start | bytes 442372
  4.5 0.9 %copy-start.3 = (f32[24,12,128]{2,0,1:T(8,128)S(1)}, f32[24,12,128]{2,0,1:T(8,128)}, u32[]{:S(2)}) copy-start(f32[24,12,128]{2,0,1:T(8,128)} %param.13) | copy-start | bytes 442372
  5.4 0.8 %copy-start.4 = (f32[12,1024]{1,0:T(8,128)S(1)}, f32[12,1024]{1,0:T(8,128)}, u32[]{:S(2)}) copy-start(f32[12,1024]{1,0:T(8,128)} %upper.1) | copy-start | bytes 147460
  6.3 0.8 %copy-start.5 = (f32[12,1024]{1,0:T(8,128)S(1)}, f32[12,1024]{1,0:T(8,128)}, u32[]{:S(2)}) copy-start(f32[12,1024]{1,0:T(8,128)} %annual_cap.1) | copy-start | bytes 147460
  7.1 0.7 %copy-start.8 = (f32[32]{0:T(128)S(1)}, f32[32]{0:T(128)}, u32[]{:S(2)}) copy-start(f32[32]{0:T(128)} %param.17) | copy-start | bytes 388

commit v2 on v1

--- a/solution.py
+++ b/solution.py
@@ -41,6 +41,20 @@
 def kernel(
     time_count,
     group_count,
+    cost_far,
+    demand_far,
+    conversion_far,
+    upper_far,
+    decay_far,
+    energy_cap_far,
+    annual_cap_far,
+    line_ends_far,
+    line_cap_far,
+    primal_out,
+    flows_out,
+    prices_out,
+    storage_out,
+    year_out,
     cost,
     demand,
     conversion,
@@ -50,11 +64,6 @@
     annual_cap,
     line_ends,
     line_cap,
-    primal_out,
-    flows_out,
-    prices_out,
-    storage_out,
-    year_out,
     conv_high,
     conv_low,
     bar_high,
@@ -77,18 +86,17 @@
     inflow_recv,
     first_send,
     first_recv,
-    spread_send,
-    spread_recv,
-    turn_send,
-    turn_recv,
-    again_send,
-    again_recv,
-    last_send,
-    last_recv,
+    carry_send,
+    carry_recv,
+    part_send,
+    part_recv,
+    whole_send,
+    whole_recv,
     send_sem,
     recv_sem,
     group_send_sem,
     group_recv_sem,
+    load_sem,
 ):
     me = lax.axis_index("tm")
     group = lax.axis_index("region")
@@ -106,6 +114,23 @@
     year_bound = math.sqrt(hours_all)
     f32 = jnp.float32
 
+    loads = {}
+    for i, (name, far, near) in enumerate(
+        (
+            ("cost", cost_far, cost),
+            ("demand", demand_far, demand),
+            ("decay", decay_far, decay),
+            ("upper", upper_far, upper),
+            ("conversion", conversion_far, conversion),
+            ("energy_cap", energy_cap_far, energy_cap),
+            ("annual_cap", annual_cap_far, annual_cap),
+            ("line_ends", line_ends_far, line_ends),
+            ("line_cap", line_cap_far, line_cap),
+        )
+    ):
+        loads[name] = pltpu.make_async_copy(far, near, load_sem.at[i])
+        loads[name].start()
+
     barrier = pltpu.get_barrier_semaphore()
 
     def greet_time(k, _):
@@ -164,10 +189,8 @@
             part = recv.at[pl.ds(0, count - 1)]
             pltpu.make_async_copy(part, part, sem).wait()
 
-    zero_units = jnp.zeros((regions, units), f32)
-    for t in range(hours):
-        keep[t] = decay[pl.ds(t, regions, stride=hours), :]
-
+    loads["cost"].wait()
+    loads["demand"].wait()
     def square_sums(r, carry):
         a, b = carry
         for chunk in chunks:
@@ -182,6 +205,11 @@
         square_sums,
         (jnp.zeros((hours, CHUNK), f32), jnp.zeros((hours, rows_bus), f32)),
     )
+    loads["decay"].wait()
+    zero_units = jnp.zeros((regions, units), f32)
+    for t in range(hours):
+        keep[t] = decay[pl.ds(t, regions, stride=hours), :]
+
     whole_decay = lax.fori_loop(
         0, hours, lambda t, d: d * keep[t], jnp.ones((regions, units), f32)
     )
@@ -194,6 +222,16 @@
     square_recv[group] = own_squares
     pl.semaphore_wait(barrier, time_count - 1 + group_count - 1)
     send_group(0, square_recv)
+    await_bytes(square_recv, group_count, group_recv_sem.at[0])
+    squares = jnp.sum(square_recv[...], axis=0)
+    first_send[0:rows, :] = padded(whole_decay, rows)
+    first_send[rows : rows + SUBLANES, :] = squares
+    first_recv[me, 0:rows, :] = padded(whole_decay, rows)
+    first_recv[me, rows : rows + SUBLANES, :] = squares
+    send_time(0, lambda peer: first_send, first_recv)
+
+    for name in ("upper", "conversion", "energy_cap", "annual_cap", "line_ends", "line_cap"):
+        loads[name].wait()
     column = lax.broadcasted_iota(jnp.int32, (regions, width), 1)
     lower[0:regions, :] = jnp.where(column < units, -upper[...], 0.0)
     year_sum[...] = jnp.zeros_like(year_sum)
@@ -201,13 +239,6 @@
     high, low = split_in_two(conv)
     conv_high[...] = high
     conv_low[...] = low
-    await_bytes(square_recv, group_count, group_recv_sem.at[0])
-    squares = jnp.sum(square_recv[...], axis=0)
-    first_send[0:rows, :] = padded(whole_decay, rows)
-    first_send[rows : rows + SUBLANES, :] = squares
-    first_recv[me, 0:rows, :] = padded(whole_decay, rows)
-    first_recv[me, rows : rows + SUBLANES, :] = squares
-    send_time(0, lambda peer: first_send, first_recv)
 
     bus_width = bus_recv.shape[2]
     ends = line_ends[...]
@@ -255,15 +286,21 @@
 
     over_regions(first_pass)
 
-    def send_sums(phase, send, recv):
+    def send_carry(phase, at, value):
+        carry_send[at] = padded(value, rows)
+        carry_recv[at, me] = padded(value, rows)
+        send_time(phase, lambda peer: carry_send.at[at], carry_recv.at[at])
+
+    def send_levels(phase, at):
         def run_levels(t, level):
             level = keep[t] * level + charge[pl.ds(t, regions, stride=hours), :]
             levels[t] = level
             return level
 
-        level = padded(lax.fori_loop(0, hours, run_levels, zero_units, unroll=4), rows)
+        send_carry(phase, at, lax.fori_loop(0, hours, run_levels, zero_units, unroll=4))
+
+    def send_parts(phase, at):
         for owner in range(time_count):
-            send[owner, 0:rows, :] = level
             for j in range(share):
                 tile = owner * share + j
                 if tile < tiles:
@@ -274,15 +311,21 @@
                     ]
                 else:
                     part = jnp.zeros((SUBLANES, LANES), f32)
-                at = rows + j * SUBLANES
-                send[owner, at : at + SUBLANES, :] = part
-        recv[me] = send[me]
-        send_time(phase, lambda peer: send.at[peer], recv)
+                part_send[at, owner, j * SUBLANES : (j + 1) * SUBLANES, :] = part
+        part_recv[at, me] = part_send[at, me]
+        send_time(phase, lambda peer: part_send.at[at, peer], part_recv.at[at])
+
+    def send_whole(phase, at):
+        own = jnp.sum(part_recv[at], axis=0)
+        whole_send[at] = own
+        whole_recv[at, me] = own
+        send_time(phase, lambda peer: whole_send.at[at], whole_recv.at[at])
 
     def matmul_image():
         image[...] = product(bar_high[...], bar_low[...], conv_high[...], conv_low[...], 0)
 
-    send_sums(1, spread_send, spread_recv)
+    send_levels(1, 0)
+    send_parts(2, 0)
     matmul_image()
 
     def first_prices(i, bus):
@@ -306,20 +349,16 @@
     send_group(1, bus_recv)
     back[...] = product(price_high[...], price_low[...], conv_high[...], conv_low[...], 1)
 
-    await_bytes(spread_recv, time_count, recv_sem.at[1])
-
-    def carried(recv):
+    await_bytes(carry_recv.at[0], time_count, recv_sem.at[1])
+
+    def carried(at):
         def one(j, state):
-            return first_recv[j, 0:rows, :] * state + recv[j, 0:rows, :]
+            return first_recv[j, 0:rows, :] * state + carry_recv[at, j]
 
         state = lax.fori_loop(0, me, one, jnp.zeros((rows, units), f32))
         return state[0:regions]
 
-    def year_total(recv):
-        return jnp.sum(recv[:, rows:, :], axis=0)
-
-    own_year = year_total(spread_recv)
-    turn = carried(spread_recv)
+    turn = carried(0)
     caps = energy_cap[...]
 
     def first_storage(t, run):
@@ -335,11 +374,9 @@
         return keep[t] * (scale * storage[t] + run)
 
     run = lax.fori_loop(0, hours, adjoint_only, zero_units, unroll=4)
-    turn_send[0:rows, :] = padded(run, rows)
-    turn_send[rows:, :] = own_year
-    turn_recv[me, 0:rows, :] = padded(run, rows)
-    turn_recv[me, rows:, :] = own_year
-    send_time(2, lambda peer: turn_send, turn_recv)
+    send_carry(3, 1, run)
+    await_bytes(part_recv.at[0], time_count, recv_sem.at[2])
+    send_whole(4, 0)
 
     await_bytes(bus_recv, group_count, group_recv_sem.at[1])
     exact = functools.partial(
@@ -353,11 +390,11 @@
     inflow_recv[group] = exact(2.0 * flows, incidence, (((1,), (1,)), ((), ())))
     send_group(2, inflow_recv)
 
-    await_bytes(turn_recv, time_count, recv_sem.at[2])
+    await_bytes(carry_recv.at[1], time_count, recv_sem.at[3])
 
     def ahead(i, state):
         j = time_count - 1 - i
-        return first_recv[j, 0:rows, :] * state + turn_recv[j, 0:rows, :]
+        return first_recv[j, 0:rows, :] * state + carry_recv[1, j]
 
     run = lax.fori_loop(0, time_count - 1 - me, ahead, jnp.zeros((rows, units), f32))[0:regions]
 
@@ -369,20 +406,21 @@
 
     lax.fori_loop(0, hours, adjoint, run, unroll=4)
 
-    def year_parts(recv_tile):
+    def year_parts(at):
         for tile in range(tiles):
             half, block = tile // blocks, tile % blocks
             first = half * SUBLANES
             last = min(first + SUBLANES, regions)
             if last <= first:
                 continue
-            at = rows + (tile % share) * SUBLANES
-            total = recv_tile(tile // share, at)[0 : last - first]
+            down = (tile % share) * SUBLANES
+            total = whole_recv[at, tile // share, down : down + last - first, :]
             cap = annual_cap[first:last, block * LANES : (block + 1) * LANES]
             step = sigma * (scale * total - year_bound * cap)
             yield slice(first, last), slice(block * LANES, (block + 1) * LANES), step
 
-    for r, c, step in year_parts(lambda owner, at: turn_recv[owner, at : at + SUBLANES, :]):
+    await_bytes(whole_recv.at[0], time_count, recv_sem.at[4])
+    for r, c, step in year_parts(0):
         year_dual[r, c] = jnp.maximum(step, 0.0)
 
     def second_pass(r, chunk):
@@ -399,7 +437,8 @@
         return bar
 
     over_regions(second_pass)
-    send_sums(3, again_send, again_recv)
+    send_parts(5, 1)
+    send_levels(6, 2)
     matmul_image()
     await_bytes(inflow_recv, group_count, group_recv_sem.at[2])
     inflow = jnp.sum(inflow_recv[...], axis=0)
@@ -414,12 +453,10 @@
 
     lax.fori_loop(0, regions, second_prices, 0)
 
-    await_bytes(again_recv, time_count, recv_sem.at[3])
-    own_year = year_total(again_recv)
-    last_send[...] = own_year
-    last_recv[me] = own_year
-    send_time(4, lambda peer: last_send, last_recv)
-    turn = carried(again_recv)
+    await_bytes(part_recv.at[1], time_count, recv_sem.at[5])
+    send_whole(7, 1)
+    await_bytes(carry_recv.at[2], time_count, recv_sem.at[6])
+    turn = carried(2)
 
     def second_storage(t, run):
         run = keep[t] * run
@@ -429,13 +466,21 @@
         return run
 
     lax.fori_loop(0, hours, second_storage, turn, unroll=4)
-    await_bytes(last_recv, time_count, recv_sem.at[4])
-    for r, c, step in year_parts(
-        lambda owner, at: last_recv[owner, at - rows : at - rows + SUBLANES, :]
-    ):
+    await_bytes(whole_recv.at[1], time_count, recv_sem.at[7])
+    for r, c, step in year_parts(1):
         year_out[r, c] = jnp.maximum(year_dual[r, c] + step, 0.0)
 
-    for phase, recv in enumerate((first_recv, spread_recv, turn_recv, again_recv, last_recv)):
+    sent = (
+        first_recv,
+        carry_recv.at[0],
+        part_recv.at[0],
+        carry_recv.at[1],
+        whole_recv.at[0],
+        part_recv.at[1],
+        carry_recv.at[2],
+        whole_recv.at[1],
+    )
+    for phase, recv in enumerate(sent):
         await_bytes(recv, time_count, send_sem.at[phase])
     for phase, recv in enumerate((square_recv, bus_recv, inflow_recv)):
         await_bytes(recv, group_count, group_send_sem.at[phase])
@@ -491,6 +536,18 @@
     half = lambda *shape: pltpu.VMEM(shape, bf16)
     flat = hours * regions
     by_region = lambda x: jnp.transpose(x, (1, 0, 2))
+    operands = (
+        by_region(cost),
+        by_region(demand),
+        conversion,
+        upper,
+        by_region(decay).reshape(flat, units),
+        energy_cap,
+        annual_cap,
+        line_ends.T,
+        line_cap.reshape(1, lines),
+    )
+    operands = tuple(pltpu.with_memory_space_constraint(x, pltpu.HBM) for x in operands)
     results = pl.pallas_call(
         functools.partial(kernel, time_count, group_count),
         out_shape=(
@@ -500,9 +557,10 @@
             jax.ShapeDtypeStruct((flat, units), f32),
             jax.ShapeDtypeStruct((regions, width), f32),
         ),
-        in_specs=[vmem] * 9,
+        in_specs=[pl.BlockSpec(memory_space=pltpu.HBM)] * len(operands),
         out_specs=[vmem] * 5,
-        scratch_shapes=[
+        scratch_shapes=[pltpu.VMEM(x.shape, x.dtype) for x in operands]
+        + [
             half(width, rows_bus),
             half(width, rows_bus),
             half(flat, width),
@@ -525,33 +583,22 @@
             scratch(group_count, hours, bus_width),
             scratch(rows + SUBLANES, units),
             scratch(time_count, rows + SUBLANES, units),
-            scratch(time_count, rows + share, units),
-            scratch(time_count, rows + share, units),
-            scratch(rows + share, units),
-            scratch(time_count, rows + share, units),
-            scratch(time_count, rows + share, units),
-            scratch(time_count, rows + share, units),
-            scratch(share, units),
-            scratch(time_count, share, units),
-            pltpu.SemaphoreType.DMA((5,)),
-            pltpu.SemaphoreType.DMA((5,)),
+            scratch(3, rows, units),
+            scratch(3, time_count, rows, units),
+            scratch(2, time_count, share, LANES),
+            scratch(2, time_count, share, LANES),
+            scratch(2, share, LANES),
+            scratch(2, time_count, share, LANES),
+            pltpu.SemaphoreType.DMA((8,)),
+            pltpu.SemaphoreType.DMA((8,)),
             pltpu.SemaphoreType.DMA((3,)),
             pltpu.SemaphoreType.DMA((3,)),
+            pltpu.SemaphoreType.DMA((9,)),
         ],
         compiler_params=pltpu.CompilerParams(
             collective_id=0, has_side_effects=True, vmem_limit_bytes=20 * 2**20
         ),
-    )(
-        by_region(cost),
-        by_region(demand),
-        conversion,
-        upper,
-        by_region(decay).reshape(flat, units),
-        energy_cap,
-        annual_cap,
-        line_ends.T,
-        line_cap.reshape(1, lines),
-    )
+    )(*operands)
     primal, flows, prices, storage, year = delivered(results)
     return (
         by_region(primal),

time: 48.1 us -> 39.6 us (0.82)
  local copies, waits for them, and re-layouts: 7.12 us -> 0 us
  Pallas kernels: 40 us -> 38.8 us
    unnamed x18 -> x0, local copies, waits for them, and re-layouts: 7.12 us -> none
    pallas_call x1, Pallas kernels: 38.9 us -> 37.8 us  [per_device(): pl.pallas_call(functools.partial(kernel, time_count, group_count), out_sh...]
where the time goes in v2:
time: 39.6 us; the launch traced here: 39.5 us
  Pallas kernels  38.8 us (98%)
  between operations  0.64 us (2%)
    pallas_call x1, Pallas kernels, per_device(): pl.pallas_call(functools.partial(kernel, time_count, group_count), out_sh...  37.8 us
    pallas_call x1, Pallas kernels, delivered(): pl.pallas_call(deliver, out_shape=tuple((jax.ShapeDtypeStruct(a.shape, a....  1.02 us

profile of v2, /device:TPU:0, one launch (start us, length us, event | category | flops | bytes accessed | tf_op | source)
XLA Modules:
  0.0 39.5 jit_solution(10013641557642357516)
XLA Ops:
  0.6 37.8 %shard_map.128 = (bf16[12,24,1024]{2,1,0:T(8,128)(2,1)S(1)}, f32[24,32]{1,0:T(8,128)S(1)}, f32[12,24,256]{2,1,0:T(8,128)S(1)}, f32[288,128]{1,0:T(8,128)S(1)}, f32[12,1024]{1,0:T(8,128)S(1)}) custom-call(bf16[12,24,1024]{2,1,0:T(8,128)(2,1)} %bitcast.12, bf16[12,24,256]{2,1,0:T(8,128)(2,1)} %bitcast.13, f32[1024,256]{1,0:T(8,128)} %conversion_far.1, ...), custom_call_target="tpu_custom_call" | custom-call | tf_op jit(solution)/shard_map/pallas_call | solution.py:551
  38.5 1.0 %shard_map.129 = (bf16[12,24,1024]{2,1,0:T(8,128)(2,1)}, f32[24,32]{1,0:T(8,128)}, f32[12,24,256]{2,1,0:T(8,128)}, f32[288,128]{1,0:T(8,128)}, f32[12,1024]{1,0:T(8,128)}) custom-call(bf16[12,24,1024]{2,1,0:T(8,128)(2,1)S(1)} %get-tuple-element.15.refs_0_, f32[24,32]{1,0:T(8,128)S(1)} %get-tuple-element.16.refs_1_, ...), custom_call_target="tpu_custom_call" | custom-call | tf_op jit(solution)/shard_map/pallas_call | solution.py:502

commit v3 on v2

--- a/solution.py
+++ b/solution.py
@@ -133,27 +133,31 @@
 
     barrier = pltpu.get_barrier_semaphore()
 
-    def greet_time(k, _):
+    everyone = time_count * group_count
+    mine = me * group_count + group
+
+    def other(k):
+        flat = lax.rem(mine + k, everyone)
+        return {"tm": flat // group_count, "region": lax.rem(flat, group_count)}
+
+    def greet(k, _):
         pl.semaphore_signal(
-            barrier,
-            inc=1,
-            device_id={"tm": lax.rem(me + k, time_count)},
-            device_id_type=pl.DeviceIdType.MESH,
+            barrier, inc=1, device_id=other(k), device_id_type=pl.DeviceIdType.MESH
         )
         return 0
 
-    lax.fori_loop(1, time_count, greet_time, 0)
-
-    def greet_group(k, _):
-        pl.semaphore_signal(
-            barrier,
-            inc=1,
-            device_id={"region": lax.rem(group + k, group_count)},
+    lax.fori_loop(1, everyone, greet, 0)
+
+    def send_squares(k, _):
+        pltpu.make_async_remote_copy(
+            src_ref=square_recv.at[mine],
+            dst_ref=square_recv.at[mine],
+            send_sem=group_send_sem.at[0],
+            recv_sem=group_recv_sem.at[0],
+            device_id=other(k),
             device_id_type=pl.DeviceIdType.MESH,
-        )
+        ).start()
         return 0
-
-    lax.fori_loop(1, group_count, greet_group, 0)
 
     def send_time(phase, source_of, recv):
         def one(k, _):
@@ -205,6 +209,14 @@
         square_sums,
         (jnp.zeros((hours, CHUNK), f32), jnp.zeros((hours, rows_bus), f32)),
     )
+    def total(x):
+        return jnp.sum(jnp.sum(x, axis=0, keepdims=True), axis=1, keepdims=True)
+
+    lane = lax.broadcasted_iota(jnp.int32, (1, LANES), 1)
+    square_recv[mine] = jnp.where(lane == 0, total(a), total(b))
+    pl.semaphore_wait(barrier, everyone - 1)
+    lax.fori_loop(1, everyone, send_squares, 0)
+
     loads["decay"].wait()
     zero_units = jnp.zeros((regions, units), f32)
     for t in range(hours):
@@ -214,20 +226,8 @@
         0, hours, lambda t, d: d * keep[t], jnp.ones((regions, units), f32)
     )
 
-    def folded(x):
-        x = jnp.sum(x, axis=0, keepdims=True)
-        return sum(x[:, i * LANES : (i + 1) * LANES] for i in range(x.shape[1] // LANES))
-
-    own_squares = padded(jnp.concatenate([folded(a), folded(b)], axis=0), SUBLANES)
-    square_recv[group] = own_squares
-    pl.semaphore_wait(barrier, time_count - 1 + group_count - 1)
-    send_group(0, square_recv)
-    await_bytes(square_recv, group_count, group_recv_sem.at[0])
-    squares = jnp.sum(square_recv[...], axis=0)
-    first_send[0:rows, :] = padded(whole_decay, rows)
-    first_send[rows : rows + SUBLANES, :] = squares
-    first_recv[me, 0:rows, :] = padded(whole_decay, rows)
-    first_recv[me, rows : rows + SUBLANES, :] = squares
+    first_send[...] = padded(whole_decay, rows)
+    first_recv[me] = padded(whole_decay, rows)
     send_time(0, lambda peer: first_send, first_recv)
 
     for name in ("upper", "conversion", "energy_cap", "annual_cap", "line_ends", "line_cap"):
@@ -246,10 +246,10 @@
     incidence = (ends[1:2, :] == region_id).astype(f32) - (ends[0:1, :] == region_id).astype(f32)
     spot = lax.broadcasted_iota(jnp.int32, (hours, bus_width), 1) - group * regions
 
-    await_bytes(first_recv, time_count, recv_sem.at[0])
-    squares = jnp.sum(first_recv[:, rows : rows + SUBLANES, :], axis=0)
-    sums = jnp.sum(squares, axis=1, keepdims=True)
-    omega = jnp.sqrt(sums[0:1] / sums[1:2])
+    await_bytes(square_recv, everyone, group_recv_sem.at[0])
+    squares = jnp.sum(square_recv[...], axis=0)
+    sums = squares[:, 0:1], squares[:, 1:2]
+    omega = jnp.sqrt(sums[0] / sums[1])
     tau = step_ratio / omega
     sigma = step_ratio * omega
 
@@ -349,11 +349,12 @@
     send_group(1, bus_recv)
     back[...] = product(price_high[...], price_low[...], conv_high[...], conv_low[...], 1)
 
+    await_bytes(first_recv, time_count, recv_sem.at[0])
     await_bytes(carry_recv.at[0], time_count, recv_sem.at[1])
 
     def carried(at):
         def one(j, state):
-            return first_recv[j, 0:rows, :] * state + carry_recv[at, j]
+            return first_recv[j] * state + carry_recv[at, j]
 
         state = lax.fori_loop(0, me, one, jnp.zeros((rows, units), f32))
         return state[0:regions]
@@ -394,7 +395,7 @@
 
     def ahead(i, state):
         j = time_count - 1 - i
-        return first_recv[j, 0:rows, :] * state + carry_recv[1, j]
+        return first_recv[j] * state + carry_recv[1, j]
 
     run = lax.fori_loop(0, time_count - 1 - me, ahead, jnp.zeros((rows, units), f32))[0:regions]
 
@@ -482,8 +483,9 @@
     )
     for phase, recv in enumerate(sent):
         await_bytes(recv, time_count, send_sem.at[phase])
-    for phase, recv in enumerate((square_recv, bus_recv, inflow_recv)):
-        await_bytes(recv, group_count, group_send_sem.at[phase])
+    await_bytes(square_recv, everyone, group_send_sem.at[0])
+    await_bytes(bus_recv, group_count, group_send_sem.at[1])
+    await_bytes(inflow_recv, group_count, group_send_sem.at[2])
 
 
 def deliver(*refs):
@@ -578,11 +580,11 @@
             scratch(rows, width),
             scratch(rows, width),
             scratch(rows, width),
-            scratch(group_count, SUBLANES, LANES),
+            scratch(time_count * group_count, 1, LANES),
             scratch(group_count, hours, bus_width),
             scratch(group_count, hours, bus_width),
-            scratch(rows + SUBLANES, units),
-            scratch(time_count, rows + SUBLANES, units),
+            scratch(rows, units),
+            scratch(time_count, rows, units),
             scratch(3, rows, units),
             scratch(3, time_count, rows, units),
             scratch(2, time_count, share, LANES),

time: 39.6 us -> 37 us (0.934)
  Pallas kernels: 38.8 us -> 36.2 us
    pallas_call x1, Pallas kernels: 37.8 us -> 35.2 us  [per_device(): pl.pallas_call(functools.partial(kernel, time_count, group_count), out_sh...]
where the time goes in v3:
time: 37 us; the launch traced here: 36.8 us
  Pallas kernels  36.2 us (98%)
  between operations  0.64 us (2%)
    pallas_call x1, Pallas kernels, per_device(): pl.pallas_call(functools.partial(kernel, time_count, group_count), out_sh...  35.2 us
    pallas_call x1, Pallas kernels, delivered(): pl.pallas_call(deliver, out_shape=tuple((jax.ShapeDtypeStruct(a.shape, a....  1.02 us

profile of v3, /device:TPU:0, one launch (start us, length us, event | category | flops | bytes accessed | tf_op | source)
XLA Modules:
  0.0 36.8 jit_solution(13627651398517825227)
XLA Ops:
  0.6 35.2 %shard_map.128 = (bf16[12,24,1024]{2,1,0:T(8,128)(2,1)S(1)}, f32[24,32]{1,0:T(8,128)S(1)}, f32[12,24,256]{2,1,0:T(8,128)S(1)}, f32[288,128]{1,0:T(8,128)S(1)}, f32[12,1024]{1,0:T(8,128)S(1)}) custom-call(bf16[12,24,1024]{2,1,0:T(8,128)(2,1)} %bitcast.12, bf16[12,24,256]{2,1,0:T(8,128)(2,1)} %bitcast.13, f32[1024,256]{1,0:T(8,128)} %conversion_far.1, ...), custom_call_target="tpu_custom_call" | custom-call | tf_op jit(solution)/shard_map/pallas_call | solution.py:553
  35.8 1.0 %shard_map.129 = (bf16[12,24,1024]{2,1,0:T(8,128)(2,1)}, f32[24,32]{1,0:T(8,128)}, f32[12,24,256]{2,1,0:T(8,128)}, f32[288,128]{1,0:T(8,128)}, f32[12,1024]{1,0:T(8,128)}) custom-call(bf16[12,24,1024]{2,1,0:T(8,128)(2,1)S(1)} %get-tuple-element.15.refs_0_, f32[24,32]{1,0:T(8,128)S(1)} %get-tuple-element.16.refs_1_, ...), custom_call_target="tpu_custom_call" | custom-call | tf_op jit(solution)/shard_map/pallas_call | solution.py:504
